TPU v7x, 32 devices: a whole 2x2x4 slice. The times are simulated.
32 devices in a mesh: dp: 8 (over z, y), tensor: 4 (over x, core).
Axes of the slice: x: 2, y: 2, z: 4, core: 2. Of those that a mesh axis runs over, the one named last changes fastest.
Arguments:
- hidden: bfloat16 [12288, 1536], P('dp'), may hold values from -6 to 6
- segment_ids: int32 [12288], P('dp'), may hold values from -1 to 12287, as said below
- norm_gain: float32 [1536], replicated, may hold values from 0.5 to 1.5
- gate_weight: bfloat16 [1536, 3072], P(None, 'tensor'), may hold values from -0.15625 to 0.15625
- input_weight: bfloat16 [1536, 3072], P(None, 'tensor'), may hold values from -0.15625 to 0.15625
- step_weight: bfloat16 [1536, 48], P(None, 'tensor'), may hold values from -0.15625 to 0.15625
- state_weight: bfloat16 [1536, 256], replicated, may hold values from -0.15625 to 0.15625
- conv_weight: float32 [4, 3072], P(None, 'tensor'), may hold values from -3 to 3
- state_conv_weight: float32 [4, 256], replicated, may hold values from -3 to 3
- conv_bias: float32 [3072], P('tensor'), may hold values from -0.5 to 0.5
- state_conv_bias: float32 [256], replicated, may hold values from -0.5 to 0.5
- step_bias: float32 [48], P('tensor'), may hold values from -6.9 to -2.25
- decay_log: float32 [48], P('tensor'), may hold values from 0 to 2.77
- skip_gain: float32 [48], P('tensor'), may hold values from 0.5 to 1.5
- gate_norm_gain: float32 [3072], P('tensor'), may hold values from 0.5 to 1.5
- out_weight: bfloat16 [3072, 1536], P('tensor'), may hold values from -0.109375 to 0.109375
- cotangent: bfloat16 [12288, 1536], P('dp'), may hold values from -6 to 6
Outputs:
- block_out: bfloat16 [12288, 1536], P('dp')
- grad_hidden: float32 [12288, 1536], P('dp')
- grad_norm_gain: float32 [1536], replicated
- grad_gate_weight: float32 [1536, 3072], P(None, 'tensor')
- grad_input_weight: float32 [1536, 3072], P(None, 'tensor')
- grad_step_weight: float32 [1536, 48], P(None, 'tensor')
- grad_state_weight: float32 [1536, 256], replicated
- grad_conv_weight: float32 [4, 3072], P(None, 'tensor')
- grad_state_conv_weight: float32 [4, 256], replicated
- grad_conv_bias: float32 [3072], P('tensor')
- grad_state_conv_bias: float32 [256], replicated
- grad_step_bias: float32 [48], P('tensor')
- grad_decay_log: float32 [48], P('tensor')
- grad_skip_gain: float32 [48], P('tensor')
- grad_gate_norm_gain: float32 [3072], P('tensor')
- grad_out_weight: float32 [3072, 1536], P('tensor')
Inputs may be any that keep to these rules, and one draw needn't show every extreme that they name: `segment_ids`: each value is -1 for an empty slot or the global index of the first slot of its sequence; a sequence lies within the 1536 slots of one dp index, its slots are consecutive; the empty slots of a dp index come after all its sequences and number a multiple of 256; the last dp index has no empty slot, and the last slot of all starts a sequence of one token.
All inputs are finite; a program needn't handle non-finite values.
Results may differ from a plain program's by a relative error of at most 0.0096.
Values may be sent and summed in bfloat16 or wider, within the bound.
No kernel may reach another device: no remote copies, remote signals or barrier semaphores. Data moves between devices by JAX's collectives and lax.ppermute only.
A program may use at most 256 MiB of HBM per device.

v0:
```python
from functools import partial
import jax
import jax.numpy as jnp
from jax import lax
from jax.sharding import PartitionSpec as P

INNER = 3072
GROUP = 256
EPS = 1e-05
HIGH = lax.Precision.HIGHEST


def conv_silu(inputs, weights, biases, segments):
    summed = biases[None, :] + weights[0][None, :] * inputs
    for offset in range(1, weights.shape[0]):
        shifted = jnp.concatenate(
            [jnp.zeros((offset, inputs.shape[1]), inputs.dtype), inputs[:-offset]], axis=0
        )
        seg_shift = jnp.concatenate([jnp.full((offset,), -2, jnp.int32), segments[:-offset]])
        keeping = (seg_shift == segments).astype(inputs.dtype)
        summed = summed + weights[offset][None, :] * shifted * keeping[:, None]
    return jax.nn.silu(summed)


def ssd_scan(values, states, step_raw, step_bias, decay_log, skip_gain, segments, group):
    length = values.shape[0]
    heads = step_bias.shape[0]
    width = values.shape[1] // heads
    state = states.shape[1] // 2
    blocks = length // group
    step = jax.nn.softplus(step_raw + step_bias[None, :])
    rate = step * (-jnp.exp(decay_log))[None, :]
    x_blk = values.reshape(blocks, group, heads, width)
    b_blk = states[:, :state].reshape(blocks, group, state)
    c_blk = states[:, state:].reshape(blocks, group, state)
    step_h = step.reshape(blocks, group, heads).transpose(0, 2, 1)
    cum_h = jnp.cumsum(rate.reshape(blocks, group, heads), axis=1).transpose(0, 2, 1)
    seg_blk = segments.reshape(blocks, group)
    causal = jnp.tril(jnp.ones((group, group), bool))
    same = ((seg_blk[:, :, None] == seg_blk[:, None, :]) & causal[None])[:, None]
    differ = cum_h[:, :, :, None] - cum_h[:, :, None, :]
    decay = jnp.where(same, jnp.exp(jnp.where(same, differ, 0.0)), 0.0)
    inner_cb = jnp.einsum("cin,cjn->cij", c_blk, b_blk, precision=HIGH)
    mixing = decay * inner_cb[:, None] * step_h[:, :, None, :]
    y_diag = jnp.einsum("chij,cjhp->cihp", mixing, x_blk, precision=HIGH)
    last_seg = seg_blk[:, -1]
    to_end = jnp.exp(cum_h[:, :, -1:] - cum_h) * step_h * (seg_blk == last_seg[:, None])[:, None, :]
    weighted = to_end.transpose(0, 2, 1)[..., None] * x_blk
    local_state = jnp.einsum("cjn,cjhp->chnp", b_blk, weighted, precision=HIGH)
    prev_seg = jnp.concatenate([jnp.full((1,), -3, jnp.int32), last_seg[:-1]])
    carry_keep = (last_seg == prev_seg).astype(values.dtype)[:, None] * jnp.exp(cum_h[:, :, -1])

    def advance(entering, pieces):
        local_part, factor = pieces
        return (local_part + factor[:, None, None] * entering, entering)

    start_state = jnp.zeros((heads, state, width), values.dtype)
    _, entering_all = lax.scan(advance, start_state, (local_state, carry_keep))
    reach = jnp.exp(cum_h).transpose(0, 2, 1) * (seg_blk == prev_seg[:, None])[..., None]
    y_off = jnp.einsum("cin,chnp->cihp", c_blk, entering_all, precision=HIGH) * reach[..., None]
    result = y_diag + y_off + skip_gain[None, None, :, None] * x_blk
    return result.reshape(length, heads * width)


def cross_dot(left, right):
    return lax.dot_general(
        left, right, (((0,), (0,)), ((), ())), preferred_element_type=jnp.float32
    )


def back_dot(left, right):
    return lax.dot_general(
        left, right, (((1,), (1,)), ((), ())), preferred_element_type=jnp.float32
    )


def body(
    hidden,
    segment_ids,
    norm_gain,
    gate_weight,
    input_weight,
    step_weight,
    state_weight,
    conv_weight,
    state_conv_weight,
    conv_bias,
    state_conv_bias,
    step_bias,
    decay_log,
    skip_gain,
    gate_norm_gain,
    out_weight,
    cotangent,
):
    valid = (segment_ids >= 0).astype(jnp.float32)[:, None]
    hidden_f = hidden.astype(jnp.float32)
    inverse = lax.rsqrt(jnp.mean(hidden_f * hidden_f, axis=1, keepdims=True) + EPS)
    normed = (hidden_f * inverse * norm_gain[None, :]).astype(jnp.bfloat16)
    gate_pre = jnp.dot(normed, gate_weight, preferred_element_type=jnp.float32)
    input_pre = jnp.dot(normed, input_weight, preferred_element_type=jnp.float32)
    step_pre = jnp.dot(normed, step_weight, preferred_element_type=jnp.float32)
    state_pre = jnp.dot(normed, state_weight, preferred_element_type=jnp.float32)
    conv_out, conv_back = jax.vjp(
        partial(conv_silu, segments=segment_ids), input_pre, conv_weight, conv_bias
    )
    state_out, state_back = jax.vjp(
        partial(conv_silu, segments=segment_ids), state_pre, state_conv_weight, state_conv_bias
    )
    values_f = lax.optimization_barrier(conv_out.astype(jnp.bfloat16)).astype(jnp.float32)
    states_f = lax.optimization_barrier(state_out.astype(jnp.bfloat16)).astype(jnp.float32)
    mixed_y, ssd_back = jax.vjp(
        partial(ssd_scan, segments=segment_ids, group=GROUP),
        values_f,
        states_f,
        step_pre,
        step_bias,
        decay_log,
        skip_gain,
    )
    gate_act = jax.nn.silu(gate_pre)
    gated = mixed_y * gate_act
    square_sum = lax.psum(jnp.sum(gated * gated, axis=1), "tensor")
    gate_inverse = lax.rsqrt(square_sum / INNER + EPS)[:, None]
    gnormed = (gated * gate_inverse * gate_norm_gain[None, :]).astype(jnp.bfloat16)
    partial_mix = jnp.dot(gnormed, out_weight, preferred_element_type=jnp.float32)
    mix = lax.psum(partial_mix, "tensor")
    block_out = (hidden_f + valid * mix).astype(jnp.bfloat16)
    dmix = (cotangent.astype(jnp.float32) * valid).astype(jnp.bfloat16)
    grad_out = cross_dot(gnormed, dmix)
    d_gn = back_dot(dmix, out_weight)
    grad_gnorm = jnp.sum(d_gn * gated * gate_inverse, axis=0)
    scaled = d_gn * gate_norm_gain[None, :]
    dot_sum = lax.psum(jnp.sum(gated * scaled, axis=1), "tensor")
    d_gated = gate_inverse * scaled - gated * gate_inverse**3 * (dot_sum / INNER)[:, None]
    d_y = d_gated * gate_act
    sigma = jax.nn.sigmoid(gate_pre)
    d_gate = d_gated * mixed_y * sigma * (1.0 + gate_pre * (1.0 - sigma))
    d_values, d_states, d_step, grad_sbias, grad_decay, grad_skip = ssd_back(d_y)
    d_input, grad_conv, grad_cbias = conv_back(d_values)
    gate_b = d_gate.astype(jnp.bfloat16)
    input_b = d_input.astype(jnp.bfloat16)
    step_b = d_step.astype(jnp.bfloat16)
    local_back = (
        back_dot(gate_b, gate_weight)
        + back_dot(input_b, input_weight)
        + back_dot(step_b, step_weight)
    )
    summed_back, states_full = lax.psum((local_back, d_states), "tensor")
    d_state_pre, grad_sconv, grad_scbias = state_back(states_full)
    state_b = d_state_pre.astype(jnp.bfloat16)
    d_normed = summed_back + back_dot(state_b, state_weight)
    grad_norm = jnp.sum(d_normed * hidden_f * inverse, axis=0)
    scaled_in = d_normed * norm_gain[None, :]
    grad_hidden = (
        cotangent.astype(jnp.float32)
        + inverse * scaled_in
        - hidden_f * inverse**3 * jnp.mean(hidden_f * scaled_in, axis=1, keepdims=True)
    )
    grad_gate = cross_dot(normed, gate_b)
    grad_input = cross_dot(normed, input_b)
    grad_step = cross_dot(normed, step_b)
    grad_state = cross_dot(normed, state_b)
    summed = lax.psum(
        (
            grad_norm,
            grad_gate,
            grad_input,
            grad_step,
            grad_state,
            grad_conv,
            grad_sconv,
            grad_cbias,
            grad_scbias,
            grad_sbias,
            grad_decay,
            grad_skip,
            grad_gnorm,
            grad_out,
        ),
        "dp",
    )
    (
        grad_norm,
        grad_gate,
        grad_input,
        grad_step,
        grad_state,
        grad_conv,
        grad_sconv,
        grad_cbias,
        grad_scbias,
        grad_sbias,
        grad_decay,
        grad_skip,
        grad_gnorm,
        grad_out,
    ) = summed
    return (
        block_out,
        grad_hidden,
        grad_norm,
        grad_gate,
        grad_input,
        grad_step,
        grad_state,
        grad_conv,
        grad_sconv,
        grad_cbias,
        grad_scbias,
        grad_sbias,
        grad_decay,
        grad_skip,
        grad_gnorm,
        grad_out,
    )


def solution(mesh):
    return jax.shard_map(
        body,
        mesh=mesh,
        in_specs=(
            P("dp", None),
            P("dp"),
            P(),
            P(None, "tensor"),
            P(None, "tensor"),
            P(None, "tensor"),
            P(),
            P(None, "tensor"),
            P(),
            P("tensor"),
            P(),
            P("tensor"),
            P("tensor"),
            P("tensor"),
            P("tensor"),
            P("tensor", None),
            P("dp", None),
        ),
        out_specs=(
            P("dp", None),
            P("dp", None),
            P(),
            P(None, "tensor"),
            P(None, "tensor"),
            P(None, "tensor"),
            P(),
            P(None, "tensor"),
            P(),
            P("tensor"),
            P(),
            P("tensor"),
            P("tensor"),
            P("tensor"),
            P("tensor"),
            P("tensor", None),
        ),
        check_vma=False,
    )
```

profile of v0, /device:TPU:0, one launch (start us, length us, event | category | flops | bytes accessed | tf_op | source)
XLA Modules:
  0.0 1345.6 jit_solution(4326663023551138808)
XLA Ops:
  19.1 6.8 multiply_convert_fusion.2
  25.9 8.5 reshape.327
  34.3 8.2 reshape.326
  51.8 9.9 copy.178
  78.2 42.7 %while.34 = (s32[]{:T(128)}, f32[12,128,64]{2,1,0:T(8,128)}, f32[6,12,128,64]{3,2,1,0:T(8,128)}, f32[6,12,1,1]{1,3,2,0:T(1,128)}, f32[6,12,128,64]{2,3,1,0:T(8,128)}, /*index=5*/f32[6,12]{1,0:T(8,128)}, s32[]{:T(128)}, s32[]{:T(128)}) while((s32[]{:T(128)}, f32[12,128,64]{2,1,0:T(8,128)}, f32[6,12,128,64]{3,2,1,0:T(8,128)}, ...), condition=%wide.region_4.5_spmd.clone, body=%wide.region_3.4_spmd.clone.sunk | while | flops 393219 | bytes 4327672 | solution.py:58
  133.8 7.4 copy.176
  142.3 18.5 %fusion.40 = f32[6,256,12,64]{1,3,2,0:T(8,128)} fusion(f32[6,256,12,64]{1,3,2,0:T(8,128)} %copy.178, f32[6,256,12,64]{1,3,2,0:T(8,128)} %bitcast.225, f32[12]{0:T(128)S(1)} %copy-done.91, f32[6,256,12]{1,2,0:T(8,128)S(1)} %copy-done.30, bf16[6,256,12,64]{1,3,2,0:T(8,128)(2,1)} %copy.176, f32[6,12,256]{2,1,0:T(8,128)S(1)} %bitcast.258, ...), kind=kOutput, calls=%fused_computation.68 | convolution fusion | flops 3652190208 | bytes 18702384 | tf_op jit(solution)/shard_map/jvp(chij,cjhp->cihp)/dot_general | solution.py:45
  160.7 10.7 copy.219
  171.5 9.9 reshape.328
  181.4 10.2 multiply_reduce_fusion.11
  191.7 8.5 psum.133
  200.2 11.6 multiply_reduce_fusion.2
  217.9 12.3 multiply_reduce_fusion.3
  236.2 6.9 reshape.302
  243.1 19.8 %fusion.77 = f32[6,256,128]{2,1,0:T(8,128)} fusion(f32[6,12,128,64]{3,2,1,0:T(8,128)} %get-tuple-element.547, f32[6,256,12]{1,2,0:T(8,128)S(1)} %copy-done.30, f32[6,256,12,64]{1,0,3,2:T(8,128)} %reshape.302), kind=kOutput, calls=%fused_computation.129 | convolution fusion | flops 1813118976 | bytes 7938048 | tf_op jit(solution)/shard_map/transpose(jvp(cin,chnp->cihp))/dot_general | solution.py:60
  276.3 45.5 %while.35 = (s32[]{:T(128)}, f32[12,128,64]{2,1,0:T(8,128)}, f32[6,12,128,64]{3,2,1,0:T(8,128)}, f32[6,12]{1,0:T(8,128)}, f32[6,12,128,64]{2,3,1,0:T(8,128)}, /*...) while((s32[]{:T(128)}, f32[12,128,64]{2,1,0:T(8,128)}, ...), condition=%wide.region_12.13_spmd.clone, body=%wide.region_10.12_spmd.clone.sunk | while | flops 589816 | bytes 4719024 | solution.py:58
  321.8 18.7 %fusion.80 = f32[6,256,128]{2,1,0:T(8,128)S(1)} fusion(f32[6,12,128,64]{3,2,1,0:T(8,128)} %get-tuple-element.193, f32[6,256,12,64]{1,3,2,0:T(8,128)} %copy.178, f32[6,256,12]{1,2,0:T(8,128)} %copy-done.28), kind=kOutput, calls=%fused_computation.130 | convolution fusion | flops 1813118976 | bytes 7938048 | tf_op jit(solution)/shard_map/transpose(jvp(cjn,cjhp->chnp))/dot_general | solution.py:49
  340.6 8.7 multiply_reduce_fusion.9
  349.4 6.8 fusion.106
  356.2 23.7 %fusion.11 = (f32[6,12,256]{2,1,0:T(8,128)}, f32[6,12,256]{2,1,0:T(8,128)}, f32[6,12,256]{2,1,0:T(8,128)}, f32[6,256,256]{2,1,0:T(8,128)S(1)}) fusion(f32[6,12,256]{2,1,0:T(8,128)S(1)} %bitcast.259, f32[6,256,256]{2,1,0:T(8,128)S(1)} %copy-done.26, f32[6,12,256]{2,1,0:T(8,128)S(1)} %copy-done.25, pred[6,256,256]{2,1,0:T(8,128)(4,1)S(1)} %copy-done.35, ...), kind=kOutput, calls=%fused_computation.31 | convolution fusion | flops 3694209024 | bytes 10985472 | tf_op jit(solution)/shard_map/transpose(jvp(chij,cjhp->cihp))/dot_general | solution.py:45
  386.4 14.9 %reduce-window.16 = f32[6,12,2,128]{3,1,2,0:T(8,128)S(1)} reduce-window(f32[6,12,2,128]{3,1,2,0:T(8,128)S(1)} %copy.201, f32[]{:T(128)} %constant.111.clone.1), window={size=1x1x1x128 pad=0_0x0_0x0_0x0_127}, to_apply=%region_19.20 | reduce-window | flops 2340864 | bytes 147460 | tf_op jit(solution)/shard_map/reduce-window.2
  401.9 24.5 %bitcast_add_fusion.2 = f32[6,256,12,64]{1,3,2,0:T(8,128)} fusion(f32[6,256,12,64]{1,3,2,0:T(8,128)} %get-tuple-element.428, f32[12]{0:T(128)} %param.34, f32[6,256,12]{1,2,0:T(8,128)S(1)} %copy-done.29, f32[6,12,256]{2,1,0:T(8,128)} %bitcast.257, f32[6,256,256]{2,1,0:T(8,128)} %fusion.119, f32[6,12,256]{2,1,0:T(8,128)S(1)} %copy-done.25, ...), kind=kOutput, calls=%fused_computation.62 | convolution fusion | flops 3652190208 | bytes 21061680 | tf_op jit(solution)/shard_map/transpose(jvp(chij,cjhp->cihp))/dot_general | solution.py:45
  426.4 10.7 copy.221
  437.2 10.0 reshape.329
  447.2 9.5 multiply_reduce_fusion.7
  486.8 9.4 fusion.124
  496.2 8.7 fusion.123
  511.6 318.8 %all-reduce.34.cloned.1.call-done = (f32[1536,1536]{1,0:T(8,128)}, f32[1536,1536]{1,0:T(8,128)}, f32[1536,256]{1,0:T(8,128)}) async-done(((f32[1536,1536]{1,0:T(8,128)}, f32[1536,1536]{1,0:T(8,128)}, f32[1536,256]{1,0:T(8,128)}), (f32[1536,1536]{1,0:T(8,128)}, f32[1536,1536]{1,0:T(8,128)}, f32[1536,256]{1,0:T(8,128)})) %all-reduce.34.cloned.1.call-update) | async-done | bytes 20447248 | tf_op jit(solution)/shard_map/psum | solution.py:127
  841.0 9.4 fusion.21
  850.4 40.7 %all-reduce.26 = (f32[1536]{0:T(1024)}, f32[4,768]{1,0:T(4,128)}, f32[4,256]{1,0:T(4,128)}, f32[768]{0:T(1024)}, f32[256]{0:T(256)}, /*index=5*/f32[12]{0:T(128)}, f32[12]{0:T(128)}, f32[12]{0:T(128)}, f32[768]{0:T(1024)}) all-reduce(f32[1536]{0:T(1024)S(1)} %get-tuple-element.309, ...), channel_id=1, replica_groups=mesh['dp'=8,'tensor'=4] {'dp'}, use_global_device_ids=true, to_apply=%region_26.27 | all-reduce | flops 7460 | bytes 59680 | tf_op jit(solution)/shard_map/psum | solution.py:164
  891.1 17.0 %fusion.13 = (f32[1536,1536]{1,0:T(8,128)}, bf16[1536,1536]{1,0:T(8,128)(2,1)}) fusion(bf16[1536,1536]{1,0:T(8,128)(2,1)} %param.37, bf16[1536,1536]{1,0:T(8,128)(2,1)} %param.21, f32[1536,1536]{1,0:T(8,128)} %get-tuple-element.429, f32[1536]{0:T(1024)S(1)} %broadcast_multiply_fusion.8, f32[1536]{0:T(1024)S(1)} %copy-done.68, f32[1536]{0:T(1024)S(1)} %copy-done.55, ...), kind=kLoop, calls=%fused_computation.35 | loop fusion | flops 25952256 | bytes 42498048 | tf_op jit(solution)/shard_map/sub | solution.py:156
  908.1 418.2 %all-reduce.32.cloned.1.call-done = (f32[1536,768]{1,0:T(8,128)}, f32[1536,768]{1,0:T(8,128)}, f32[1536,12]{0,1:T(8,128)}, f32[1536,256]{1,0:T(8,128)}, f32[768,1536]{1,0:T(8,128)}) async-done(((f32[1536,768]{1,0:T(8,128)}, f32[1536,768]{1,0:T(8,128)}, f32[1536,12]{0,1:T(8,128)}, f32[1536,256]{1,0:T(8,128)}, f32[768,1536]{1,0:T(8,128)}), (f32[1536,768]{1,0:T(8,128)}, f32[1536,768]{1,0:T(8,128)}, ...) | async-done | bytes 15802384 | tf_op jit(solution)/shard_map/psum | solution.py:164
  (416 shorter events, 230.9 us)
Async XLA Ops:
  7.2 174.3 %copy-start = (bf16[1536,768]{1,0:T(8,128)(2,1)S(1)}, bf16[1536,768]{1,0:T(8,128)(2,1)}, u32[]{:S(2)}) copy-start(bf16[1536,768]{1,0:T(8,128)(2,1)} %param.24) | copy-start | bytes 7077892
  7.2 823.2 %all-reduce.34.cloned.1.call-start = ((), (), s32[]{:S(2)}) async-start(), calls=%async_computation.1 | async-start | bytes 40894464 | tf_op jit(solution)/shard_map/psum | solution.py:127
  19.1 46.5 %copy-start.37 = (f32[1536]{0:T(1024)}, f32[1536]{0:T(1024)S(1)}, u32[]{:S(2)}) copy-start(f32[1536]{0:T(1024)S(1)} %get-tuple-element.415) | copy-start | bytes 18436
  19.1 46.5 %copy-start.39 = (f32[1536]{0:T(1024)}, f32[1536]{0:T(1024)S(1)}, u32[]{:S(2)}) copy-start(f32[1536]{0:T(1024)S(1)} %get-tuple-element.413) | copy-start | bytes 18436
  19.1 46.5 %copy-start.41 = (f32[1536]{0:T(1024)}, f32[1536]{0:T(1024)S(1)}, u32[]{:S(2)}) copy-start(f32[1536]{0:T(1024)S(1)} %get-tuple-element.414) | copy-start | bytes 18436
  34.3 8.9 copy-start.87
  51.6 19.3 %copy-start.23 = (f32[6,12,256]{2,1,0:T(8,128)}, f32[6,12,256]{2,1,0:T(8,128)S(1)}, u32[]{:S(2)}) copy-start(f32[6,12,256]{2,1,0:T(8,128)S(1)} %reduce_window_sum.39) | copy-start | bytes 221188
  51.8 19.1 %copy-start.17 = (f32[6,256,12]{1,0,2:T(8,128)}, f32[6,256,12]{1,0,2:T(8,128)S(1)}, u32[]{:S(2)}) copy-start(f32[6,256,12]{1,0,2:T(8,128)S(1)} %reshape.299) | copy-start | bytes 221188
  51.8 9.9 copy-start.31
  69.1 9.0 copy-start.10
  181.4 18.8 %copy-start.44 = (f32[768]{0:T(1024)S(1)}, f32[768]{0:T(1024)}, u32[]{:S(2)}) copy-start(f32[768]{0:T(1024)} %param.35) | copy-start | bytes 9220
  181.4 18.8 %copy-start.56 = (f32[1536]{0:T(1024)S(1)}, f32[1536]{0:T(1024)}, u32[]{:S(2)}) copy-start(f32[1536]{0:T(1024)} %get-tuple-element.412) | copy-start | bytes 18436
  243.1 19.8 %copy-start.4 = (f32[6,256,12,64]{1,0,3,2:T(8,128)S(1)}, f32[6,256,12,64]{1,0,3,2:T(8,128)}, u32[]{:S(2)}) copy-start(f32[6,256,12,64]{1,0,3,2:T(8,128)} %reshape.302) | copy-start | bytes 14155780
  321.8 18.7 %copy-start.7 = (f32[6,12,128,64]{3,2,1,0:T(8,128)S(1)}, f32[6,12,128,64]{3,2,1,0:T(8,128)}, u32[]{:S(2)}) copy-start(f32[6,12,128,64]{3,2,1,0:T(8,128)} %get-tuple-element.193) | copy-start | bytes 7077892
  321.8 18.7 %copy-start.12 = (bf16[1536,128]{1,0:T(8,128)(2,1)S(1)}, bf16[1536,128]{1,0:T(8,128)(2,1)}, u32[]{:S(2)}) copy-start(bf16[1536,128]{1,0:T(8,128)(2,1)} %copy-done.10) | copy-start | bytes 1179652
  321.8 27.5 %slice-start.12 = ((s8[4718592]{0:T(1024)(128)(4,1)}), s8[4194304]{0:T(1024)(128)(4,1)S(1)}, s32[]{:S(2)}) async-start(s8[4718592]{0:T(1024)(128)(4,1)} %bitcast.229), calls=%async_computation.14 | async-start | bytes 8388608
  340.6 15.6 %slice-start.2 = ((s8[6291456]{0:T(1024)(128)(4,1)}), s8[4194304]{0:T(1024)(128)(4,1)S(1)}, s32[]{:S(2)}) async-start(s8[6291456]{0:T(1024)(128)(4,1)} %bitcast.216), calls=%async_computation.4 | async-start | bytes 8388608
  356.2 23.7 %copy-start.14 = (f32[6,256,128]{2,1,0:T(8,128)S(1)}, f32[6,256,128]{2,1,0:T(8,128)}, u32[]{:S(2)}) copy-start(f32[6,256,128]{2,1,0:T(8,128)} %fusion.77) | copy-start | bytes 2359300
  356.2 25.5 %copy-start.9 = (bf16[1536,128]{1,0:T(8,128)(2,1)S(1)}, bf16[1536,128]{1,0:T(8,128)(2,1)}, u32[]{:S(2)}) copy-start(bf16[1536,128]{1,0:T(8,128)(2,1)} %get-tuple-element.400) | copy-start | bytes 1179652
  380.0 22.0 %copy-start.29 = (f32[6,256,12]{1,2,0:T(8,128)S(1)}, f32[6,256,12]{1,2,0:T(8,128)}, u32[]{:S(2)}) copy-start(f32[6,256,12]{1,2,0:T(8,128)} %copy-done.28) | copy-start | bytes 221188
  437.2 10.0 copy-start.38
  437.2 19.6 %slice-start = ((s8[4718592]{0:T(1024)(128)(4,1)}), s8[524288]{0:T(1024)(128)(4,1)S(1)}, s32[]{:S(2)}) async-start(s8[4718592]{0:T(1024)(128)(4,1)} %bitcast.205), calls=%async_computation.2 | async-start | bytes 1048576
  447.2 9.6 slice-start.1
  447.2 9.6 copy-start.40
  447.2 9.6 copy-start.42
  482.6 843.6 %all-reduce.32.cloned.1.call-start = ((), (), s32[]{:S(2)}) async-start(), calls=%async_computation | async-start | bytes 31653888 | tf_op jit(solution)/shard_map/psum | solution.py:164
  486.8 9.4 copy-start.21
  486.8 18.1 %slice-start.8 = ((s8[4718592]{0:T(1024)(128)(4,1)}), s8[4194304]{0:T(1024)(128)(4,1)S(1)}, s32[]{:S(2)}) async-start(s8[4718592]{0:T(1024)(128)(4,1)} %bitcast.223), calls=%async_computation.10 | async-start | bytes 8388608
  486.8 18.1 %slice-start.14 = ((s8[4718592]{0:T(1024)(128)(4,1)}), s8[4194304]{0:T(1024)(128)(4,1)S(1)}, s32[]{:S(2)}) async-start(s8[4718592]{0:T(1024)(128)(4,1)} %bitcast.231), calls=%async_computation.16 | async-start | bytes 8388608
  841.0 9.4 copy-start.85
  841.0 50.1 %copy-start.68 = (f32[1536]{0:T(1024)S(1)}, f32[1536]{0:T(1024)}, u32[]{:S(2)}) copy-start(f32[1536]{0:T(1024)} %get-tuple-element.408) | copy-start | bytes 18436
  1326.3 10.0 slice-start.16
  (82 other events, 396.5 us)
Sparse Core Ops, SparseCore 0:
  482.8 347.5 all-reduce.33
  840.2 486.0 all-reduce.31
where the time goes:
time: 1350 us
  waiting for transfers between devices  737 us (55%)
  matrix products  231 us (17%)
  local copies, waits for them, and re-layouts  161 us (12%)
  other arithmetic  145 us (11%)
  blocking collectives  55.2 us (4%)
  between operations  15.8 us (1%)
    psum x1, waiting for transfers between devices, body(): lax.psum((grad_norm, grad_gate, grad_input, grad_step, grad_state, grad_c...  418 us
    psum x1, waiting for transfers between devices, body(): mix = lax.psum(partial_mix, 'tensor')  319 us
    dot_general x3, matrix products, ssd_scan(): y_diag = jnp.einsum('chij,cjhp->cihp', mixing, x_blk, precision=HIGH)  66.6 us
    reshape x6, local copies, waits for them, and re-layouts, ssd_scan(): x_blk = values.reshape(blocks, group, heads, width)  54.7 us
    psum x1, blocking collectives, body(): lax.psum((grad_norm, grad_gate, grad_input, grad_step, grad_state, grad_c...  40.7 us
    dot_general x5, matrix products, back_dot(): lax.dot_general(left, right, (((1,), (1,)), ((), ())), preferred_element_...  36.6 us
    dot_general x3, matrix products, ssd_scan(): local_state = jnp.einsum('cjn,cjhp->chnp', b_blk, weighted, precision=HIGH)  31.2 us
    dot_general x5, matrix products, cross_dot(): lax.dot_general(left, right, (((0,), (0,)), ((), ())), preferred_element_...  31.2 us
  transfers between devices with their start and end apart: 2, of which 2 were waited for; matrix products, arithmetic and copies ran while one was open for 4% of the time, Pallas kernels for 0%

commit v1 on v0

--- a/solution.py
+++ b/solution.py
@@ -124,7 +124,10 @@
     gate_inverse = lax.rsqrt(square_sum / INNER + EPS)[:, None]
     gnormed = (gated * gate_inverse * gate_norm_gain[None, :]).astype(jnp.bfloat16)
     partial_mix = jnp.dot(gnormed, out_weight, preferred_element_type=jnp.float32)
-    mix = lax.psum(partial_mix, "tensor")
+    devices, mix = (lax.axis_size("tensor"), partial_mix)
+    for hop in [1 << k for k in range(devices.bit_length() - 1)]:
+        route = [(i, i ^ hop) for i in range(devices)]
+        mix = mix + lax.ppermute(mix, "tensor", route)
     block_out = (hidden_f + valid * mix).astype(jnp.bfloat16)
     dmix = (cotangent.astype(jnp.float32) * valid).astype(jnp.bfloat16)
     grad_out = cross_dot(gnormed, dmix)

time: 1350 us -> 1200 us (0.89)
  waiting for transfers between devices: 737 us -> 563 us
  other arithmetic: 145 us -> 160 us
    psum x1, waiting for transfers between devices: 418 us -> 250 us  [body(): lax.psum((grad_norm, grad_gate, grad_input, grad_step, grad_state, grad_c...]
    psum x1, waiting for transfers between devices: 319 us -> 160 us  [body(): summed_back, states_full = lax.psum((local_back, d_states), 'tensor')]
    ppermute x0 -> x2, waiting for transfers between devices: none -> 154 us  [body(): mix = mix + lax.ppermute(mix, 'tensor', route)]
  transfers between devices with their start and end apart: 2 -> 4, of which waited for: 2 -> 3; matrix products, arithmetic and copies ran while one was open for 4% -> 7% of each run, Pallas kernels for 0% -> 0%
where the time goes in v1:
time: 1200 us; the launch traced here: 1190 us
  waiting for transfers between devices  563 us (47%)
  matrix products  231 us (19%)
  local copies, waits for them, and re-layouts  161 us (13%)
  other arithmetic  160 us (13%)
  blocking collectives  55.6 us (5%)
  between operations  15.7 us (1%)
    psum x1, waiting for transfers between devices, body(): lax.psum((grad_norm, grad_gate, grad_input, grad_step, grad_state, grad_c...  250 us
    psum x1, waiting for transfers between devices, body(): summed_back, states_full = lax.psum((local_back, d_states), 'tensor')  160 us
    ppermute x2, waiting for transfers between devices, body(): mix = mix + lax.ppermute(mix, 'tensor', route)  154 us
    dot_general x3, matrix products, ssd_scan(): y_diag = jnp.einsum('chij,cjhp->cihp', mixing, x_blk, precision=HIGH)  66.7 us
    reshape x6, local copies, waits for them, and re-layouts, ssd_scan(): x_blk = values.reshape(blocks, group, heads, width)  54.7 us
    psum x1, blocking collectives, body(): lax.psum((grad_norm, grad_gate, grad_input, grad_step, grad_state, grad_c...  41 us
    dot_general x5, matrix products, back_dot(): lax.dot_general(left, right, (((1,), (1,)), ((), ())), preferred_element_...  36.4 us
    dot_general x3, matrix products, ssd_scan(): local_state = jnp.einsum('cjn,cjhp->chnp', b_blk, weighted, precision=HIGH)  31.2 us
  transfers between devices with their start and end apart: 4, of which 3 were waited for; matrix products, arithmetic and copies ran while one was open for 7% of the time, Pallas kernels for 0%

profile of v1, /device:TPU:0, one launch (start us, length us, event | category | flops | bytes accessed | tf_op | source)
XLA Modules:
  0.0 1187.1 jit_solution(14132665228210814893)
XLA Ops:
  25.9 8.5 reshape.327
  34.4 8.2 reshape.326
  51.8 9.9 copy.178
  78.2 42.8 %while.34 = (s32[]{:T(128)}, f32[12,128,64]{2,1,0:T(8,128)}, f32[6,12,128,64]{3,2,1,0:T(8,128)}, f32[6,12,1,1]{1,3,2,0:T(1,128)}, f32[6,12,128,64]{2,3,1,0:T(8,128)}, /*index=5*/f32[6,12]{1,0:T(8,128)}, s32[]{:T(128)}, s32[]{:T(128)}) while((s32[]{:T(128)}, f32[12,128,64]{2,1,0:T(8,128)}, f32[6,12,128,64]{3,2,1,0:T(8,128)}, ...), condition=%wide.region_4.5_spmd.clone, body=%wide.region_3.4_spmd.clone.sunk | while | flops 393219 | bytes 4327672 | solution.py:58
  133.8 7.4 copy.176
  142.3 18.5 %fusion.40 = f32[6,256,12,64]{1,3,2,0:T(8,128)} fusion(f32[6,256,12,64]{1,3,2,0:T(8,128)} %copy.178, f32[6,256,12,64]{1,3,2,0:T(8,128)} %bitcast.227, f32[12]{0:T(128)S(1)} %copy-done.90, f32[6,256,12]{1,2,0:T(8,128)S(1)} %copy-done.30, bf16[6,256,12,64]{1,3,2,0:T(8,128)(2,1)} %copy.176, f32[6,12,256]{2,1,0:T(8,128)S(1)} %bitcast.258, ...), kind=kOutput, calls=%fused_computation.68 | convolution fusion | flops 3652190208 | bytes 18702384 | tf_op jit(solution)/shard_map/jvp(chij,cjhp->cihp)/dot_general | solution.py:45
  160.8 10.7 copy.219
  171.5 9.9 reshape.328
  181.5 10.3 multiply_reduce_fusion.11
  191.8 8.5 psum.126
  200.3 11.5 multiply_reduce_fusion.2
  217.9 12.2 %multiply_reduce_fusion.3 = (f32[768]{0:T(1024)}, f32[1536,768]{1,0:T(8,128)}, bf16[1536,768]{1,0:T(8,128)(2,1)}) fusion(bf16[1536,768]{1,0:T(8,128)(2,1)} %get-tuple-element.385, f32[1536,768]{1,0:T(8,128)} %get-tuple-element.424, f32[1536]{0:T(1024)S(1)} %broadcast_multiply_fusion.7, f32[1536,768]{1,0:T(8,128)} %get-tuple-element.382, ...), kind=kLoop, calls=%fused_computation.70 | loop fusion | flops 23592192 | bytes 28336128 | tf_op jit(solution)/shard_map/transpose(jvp())/reduce_sum | solution.py:61
  236.3 6.9 reshape.302
  243.2 19.8 %fusion.77 = f32[6,256,128]{2,1,0:T(8,128)} fusion(f32[6,12,128,64]{3,2,1,0:T(8,128)} %get-tuple-element.546, f32[6,256,12]{1,2,0:T(8,128)S(1)} %copy-done.30, f32[6,256,12,64]{1,0,3,2:T(8,128)} %reshape.302), kind=kOutput, calls=%fused_computation.129 | convolution fusion | flops 1813118976 | bytes 7938048 | tf_op jit(solution)/shard_map/transpose(jvp(cin,chnp->cihp))/dot_general | solution.py:60
  276.3 45.6 %while.35 = (s32[]{:T(128)}, f32[12,128,64]{2,1,0:T(8,128)}, f32[6,12,128,64]{3,2,1,0:T(8,128)}, f32[6,12]{1,0:T(8,128)}, f32[6,12,128,64]{2,3,1,0:T(8,128)}, /*...) while((s32[]{:T(128)}, f32[12,128,64]{2,1,0:T(8,128)}, ...), condition=%wide.region_11.12_spmd.clone, body=%wide.region_9.11_spmd.clone.sunk | while | flops 589816 | bytes 4719024 | solution.py:58
  321.9 18.6 %fusion.80 = f32[6,256,128]{2,1,0:T(8,128)S(1)} fusion(f32[6,12,128,64]{3,2,1,0:T(8,128)} %get-tuple-element.193, f32[6,256,12,64]{1,3,2,0:T(8,128)} %copy.178, f32[6,256,12]{1,2,0:T(8,128)} %copy-done.28), kind=kOutput, calls=%fused_computation.130 | convolution fusion | flops 1813118976 | bytes 7938048 | tf_op jit(solution)/shard_map/transpose(jvp(cjn,cjhp->chnp))/dot_general | solution.py:49
  340.7 8.7 multiply_reduce_fusion.9
  349.5 24.1 %fusion.11 = (f32[6,12,256]{2,1,0:T(8,128)}, f32[6,12,256]{2,1,0:T(8,128)}, f32[6,12,256]{2,1,0:T(8,128)}, f32[6,256,256]{2,1,0:T(8,128)S(1)}) fusion(f32[6,12,256]{2,1,0:T(8,128)S(1)} %bitcast.259, f32[6,256,256]{2,1,0:T(8,128)S(1)} %copy-done.26, f32[6,12,256]{2,1,0:T(8,128)S(1)} %copy-done.25, pred[6,256,256]{2,1,0:T(8,128)(4,1)S(1)} %copy-done.35, ...), kind=kOutput, calls=%fused_computation.31 | convolution fusion | flops 3694209024 | bytes 10985472 | tf_op jit(solution)/shard_map/transpose(jvp(chij,cjhp->cihp))/dot_general | solution.py:45
  380.1 14.9 %reduce-window.16 = f32[6,12,2,128]{3,1,2,0:T(8,128)S(1)} reduce-window(f32[6,12,2,128]{3,1,2,0:T(8,128)S(1)} %copy.201, f32[]{:T(128)} %constant.111.clone.1), window={size=1x1x1x128 pad=0_0x0_0x0_0x0_127}, to_apply=%region_18.19 | reduce-window | flops 2340864 | bytes 147460 | tf_op jit(solution)/shard_map/reduce-window.2
  395.6 24.2 %bitcast_add_fusion.2 = f32[6,256,12,64]{1,3,2,0:T(8,128)} fusion(f32[6,256,12,64]{1,3,2,0:T(8,128)} %get-tuple-element.427, f32[12]{0:T(128)} %param.34, f32[6,256,12]{1,2,0:T(8,128)S(1)} %copy-done.29, f32[6,12,256]{2,1,0:T(8,128)} %bitcast.257, f32[6,256,256]{2,1,0:T(8,128)} %fusion.119, f32[6,12,256]{2,1,0:T(8,128)S(1)} %copy-done.25, ...), kind=kOutput, calls=%fused_computation.62 | convolution fusion | flops 3652190208 | bytes 21061680 | tf_op jit(solution)/shard_map/transpose(jvp(chij,cjhp->cihp))/dot_general | solution.py:45
  419.8 10.7 copy.221
  430.5 10.0 reshape.329
  440.5 9.7 multiply_reduce_fusion.7
  476.3 10.8 fusion.106
  491.0 8.6 fusion.124
  512.2 159.7 %all-reduce.34.cloned.1.call-done = (f32[1536,1536]{1,0:T(8,128)}, f32[1536,256]{1,0:T(8,128)}) async-done(((f32[1536,1536]{1,0:T(8,128)}, f32[1536,256]{1,0:T(8,128)}), (f32[1536,1536]{1,0:T(8,128)}, f32[1536,256]{1,0:T(8,128)})) %all-reduce.34.cloned.1.call-update) | async-done | bytes 11010064 | tf_op jit(solution)/shard_map/psum | solution.py:152
  681.8 12.8 %add.238 = f32[1536,1536]{1,0:T(8,128)} add(f32[1536,1536]{1,0:T(8,128)} %fusion.106, f32[1536,1536]{1,0:T(8,128)} %collective-permute-done) | non-fusion elementwise | flops 2359296 | bytes 28311552 | tf_op jit(solution)/shard_map/add | solution.py:130
  694.9 9.1 fusion.21
  704.1 41.0 %all-reduce.26 = (f32[1536]{0:T(1024)}, f32[4,768]{1,0:T(4,128)}, f32[4,256]{1,0:T(4,128)}, f32[768]{0:T(1024)}, f32[256]{0:T(256)}, /*index=5*/f32[12]{0:T(128)}, f32[12]{0:T(128)}, f32[12]{0:T(128)}, f32[768]{0:T(1024)}) all-reduce(f32[1536]{0:T(1024)S(1)} %get-tuple-element.309, ...), channel_id=1, replica_groups=mesh['dp'=8,'tensor'=4] {'dp'}, use_global_device_ids=true, to_apply=%region_25.26 | all-reduce | flops 7460 | bytes 59680 | tf_op jit(solution)/shard_map/psum | solution.py:167
  745.1 153.5 %collective-permute-done.1 = f32[1536,1536]{1,0:T(8,128)} collective-permute-done((f32[1536,1536]{1,0:T(8,128)}, f32[1536,1536]{1,0:T(8,128)}, u32[]{:S(2)}, u32[]{:S(2)}) %collective-permute-start.1) | collective-permute-done | bytes 9437216 | tf_op jit(solution)/shard_map/ppermute | solution.py:130
  898.6 19.3 %fusion.13 = (f32[1536,1536]{1,0:T(8,128)}, bf16[1536,1536]{1,0:T(8,128)(2,1)}) fusion(bf16[1536,1536]{1,0:T(8,128)(2,1)} %param.37, bf16[1536,1536]{1,0:T(8,128)(2,1)} %param.21, f32[1536,1536]{1,0:T(8,128)} %get-tuple-element.428, f32[1536]{0:T(1024)S(1)} %broadcast_multiply_fusion.8, f32[1536]{0:T(1024)S(1)} %copy-done.68, f32[1536]{0:T(1024)S(1)} %copy-done.55, ...), kind=kLoop, calls=%fused_computation.35 | loop fusion | flops 28311552 | bytes 51935232 | tf_op jit(solution)/shard_map/sub | solution.py:159
  917.9 249.9 %all-reduce.32.cloned.1.call-done = (f32[1536,768]{1,0:T(8,128)}, f32[1536,768]{1,0:T(8,128)}, f32[1536,12]{0,1:T(8,128)}, f32[1536,256]{1,0:T(8,128)}, f32[768,1536]{1,0:T(8,128)}) async-done(((f32[1536,768]{1,0:T(8,128)}, f32[1536,768]{1,0:T(8,128)}, f32[1536,12]{0,1:T(8,128)}, f32[1536,256]{1,0:T(8,128)}, f32[768,1536]{1,0:T(8,128)}), (f32[1536,768]{1,0:T(8,128)}, f32[1536,768]{1,0:T(8,128)}, ...) | async-done | bytes 15802384 | tf_op jit(solution)/shard_map/psum | solution.py:167
  (419 shorter events, 243.1 us)
Async XLA Ops:
  7.2 174.3 %copy-start = (bf16[1536,768]{1,0:T(8,128)(2,1)S(1)}, bf16[1536,768]{1,0:T(8,128)(2,1)}, u32[]{:S(2)}) copy-start(bf16[1536,768]{1,0:T(8,128)(2,1)} %param.24) | copy-start | bytes 7077892
  7.2 664.6 %all-reduce.34.cloned.1.call-start = ((), (), s32[]{:S(2)}) async-start(), calls=%async_computation.1 | async-start | bytes 22020096 | tf_op jit(solution)/shard_map/psum | solution.py:152
  19.0 46.5 %copy-start.37 = (f32[1536]{0:T(1024)}, f32[1536]{0:T(1024)S(1)}, u32[]{:S(2)}) copy-start(f32[1536]{0:T(1024)S(1)} %get-tuple-element.414) | copy-start | bytes 18436
  19.0 46.5 %copy-start.39 = (f32[1536]{0:T(1024)}, f32[1536]{0:T(1024)S(1)}, u32[]{:S(2)}) copy-start(f32[1536]{0:T(1024)S(1)} %get-tuple-element.412) | copy-start | bytes 18436
  19.0 46.5 %copy-start.41 = (f32[1536]{0:T(1024)}, f32[1536]{0:T(1024)S(1)}, u32[]{:S(2)}) copy-start(f32[1536]{0:T(1024)S(1)} %get-tuple-element.413) | copy-start | bytes 18436
  51.6 19.3 %copy-start.23 = (f32[6,12,256]{2,1,0:T(8,128)}, f32[6,12,256]{2,1,0:T(8,128)S(1)}, u32[]{:S(2)}) copy-start(f32[6,12,256]{2,1,0:T(8,128)S(1)} %reduce_window_sum.39) | copy-start | bytes 221188
  51.8 19.1 %copy-start.17 = (f32[6,256,12]{1,0,2:T(8,128)}, f32[6,256,12]{1,0,2:T(8,128)S(1)}, u32[]{:S(2)}) copy-start(f32[6,256,12]{1,0,2:T(8,128)S(1)} %reshape.299) | copy-start | bytes 221188
  181.5 18.8 %copy-start.44 = (f32[768]{0:T(1024)S(1)}, f32[768]{0:T(1024)}, u32[]{:S(2)}) copy-start(f32[768]{0:T(1024)} %param.35) | copy-start | bytes 9220
  181.5 18.9 %copy-start.56 = (f32[1536]{0:T(1024)S(1)}, f32[1536]{0:T(1024)}, u32[]{:S(2)}) copy-start(f32[1536]{0:T(1024)} %get-tuple-element.411) | copy-start | bytes 18436
  243.2 19.8 %copy-start.4 = (f32[6,256,12,64]{1,0,3,2:T(8,128)S(1)}, f32[6,256,12,64]{1,0,3,2:T(8,128)}, u32[]{:S(2)}) copy-start(f32[6,256,12,64]{1,0,3,2:T(8,128)} %reshape.302) | copy-start | bytes 14155780
  321.9 18.6 %copy-start.7 = (f32[6,12,128,64]{3,2,1,0:T(8,128)S(1)}, f32[6,12,128,64]{3,2,1,0:T(8,128)}, u32[]{:S(2)}) copy-start(f32[6,12,128,64]{3,2,1,0:T(8,128)} %get-tuple-element.193) | copy-start | bytes 7077892
  321.9 18.6 %copy-start.12 = (bf16[1536,128]{1,0:T(8,128)(2,1)S(1)}, bf16[1536,128]{1,0:T(8,128)(2,1)}, u32[]{:S(2)}) copy-start(bf16[1536,128]{1,0:T(8,128)(2,1)} %copy-done.10) | copy-start | bytes 1179652
  321.9 27.5 %slice-start.2 = ((s8[6291456]{0:T(1024)(128)(4,1)}), s8[4194304]{0:T(1024)(128)(4,1)S(1)}, s32[]{:S(2)}) async-start(s8[6291456]{0:T(1024)(128)(4,1)} %bitcast.216), calls=%async_computation.4 | async-start | bytes 8388608
  349.5 24.1 %copy-start.14 = (f32[6,256,128]{2,1,0:T(8,128)S(1)}, f32[6,256,128]{2,1,0:T(8,128)}, u32[]{:S(2)}) copy-start(f32[6,256,128]{2,1,0:T(8,128)} %fusion.77) | copy-start | bytes 2359300
  349.5 25.9 %copy-start.9 = (bf16[1536,128]{1,0:T(8,128)(2,1)S(1)}, bf16[1536,128]{1,0:T(8,128)(2,1)}, u32[]{:S(2)}) copy-start(bf16[1536,128]{1,0:T(8,128)(2,1)} %get-tuple-element.399) | copy-start | bytes 1179652
  373.6 22.0 %copy-start.29 = (f32[6,256,12]{1,2,0:T(8,128)S(1)}, f32[6,256,12]{1,2,0:T(8,128)}, u32[]{:S(2)}) copy-start(f32[6,256,12]{1,2,0:T(8,128)} %copy-done.28) | copy-start | bytes 221188
  430.5 10.0 copy-start.38
  430.5 19.7 %slice-start = ((s8[4718592]{0:T(1024)(128)(4,1)}), s8[524288]{0:T(1024)(128)(4,1)S(1)}, s32[]{:S(2)}) async-start(s8[4718592]{0:T(1024)(128)(4,1)} %bitcast.205), calls=%async_computation.2 | async-start | bytes 1048576
  476.1 691.8 %all-reduce.32.cloned.1.call-start = ((), (), s32[]{:S(2)}) async-start(), calls=%async_computation | async-start | bytes 31653888 | tf_op jit(solution)/shard_map/psum | solution.py:167
  476.3 14.7 %copy-start.19 = (bf16[1536,768]{1,0:T(8,128)(2,1)S(1)}, bf16[1536,768]{1,0:T(8,128)(2,1)}, u32[]{:S(2)}) copy-start(bf16[1536,768]{1,0:T(8,128)(2,1)} %get-tuple-element.390) | copy-start | bytes 7077892
  476.3 23.3 %slice-start.6 = ((s8[4718592]{0:T(1024)(128)(4,1)}), s8[524288]{0:T(1024)(128)(4,1)S(1)}, s32[]{:S(2)}) async-start(s8[4718592]{0:T(1024)(128)(4,1)} %bitcast.221), calls=%async_computation.8 | async-start | bytes 1048576
  487.2 12.5 %slice-start.7 = ((s8[4718592]{0:T(1024)(128)(4,1)}), s8[4194304]{0:T(1024)(128)(4,1)S(1)}, s32[]{:S(2)}) async-start(s8[4718592]{0:T(1024)(128)(4,1)} %bitcast.221), calls=%async_computation.9 | async-start | bytes 8388608
  487.2 194.6 %collective-permute-start = (f32[1536,1536]{1,0:T(8,128)}, f32[1536,1536]{1,0:T(8,128)}, u32[]{:S(2)}, u32[]{:S(2)}) collective-permute-start(f32[1536,1536]{1,0:T(8,128)} %fusion.106), channel_id=1, source_target_pairs={{0,1},{1,0},{2,3},{3,2},{4,5},{5,4},{6,7},{7,6},{8,9},{9,8},{10,11... | collective-permute-start | bytes 28311560 | tf_op jit(solution)/shard_map/ppermute | solution.py:130
  491.0 14.7 %slice-start.10 = ((s8[4718592]{0:T(1024)(128)(4,1)}), s8[4194304]{0:T(1024)(128)(4,1)S(1)}, s32[]{:S(2)}) async-start(s8[4718592]{0:T(1024)(128)(4,1)} %bitcast.225), calls=%async_computation.12 | async-start | bytes 8388608
  491.0 14.7 %slice-start.14 = ((s8[4718592]{0:T(1024)(128)(4,1)}), s8[4194304]{0:T(1024)(128)(4,1)S(1)}, s32[]{:S(2)}) async-start(s8[4718592]{0:T(1024)(128)(4,1)} %bitcast.231), calls=%async_computation.16 | async-start | bytes 8388608
  681.7 12.9 %copy-start.69 = (f32[768]{0:T(1024)S(1)}, f32[768]{0:T(1024)}, u32[]{:S(2)}) copy-start(f32[768]{0:T(1024)} %get-tuple-element.363) | copy-start | bytes 9220
  681.7 13.1 %copy-start.92 = (f32[12]{0:T(128)S(1)}, f32[12]{0:T(128)}, u32[]{:S(2)}) copy-start(f32[12]{0:T(128)} %param.33) | copy-start | bytes 148
  681.7 13.2 %copy-start.48 = (f32[1536]{0:T(1024)S(1)}, f32[1536]{0:T(1024)}, u32[]{:S(2)}) copy-start(f32[1536]{0:T(1024)} %copy-done.47) | copy-start | bytes 18436
  681.7 13.2 %copy-start.55 = (f32[1536]{0:T(1024)S(1)}, f32[1536]{0:T(1024)}, u32[]{:S(2)}) copy-start(f32[1536]{0:T(1024)} %param.23) | copy-start | bytes 18436
  694.6 204.0 %collective-permute-start.1 = (f32[1536,1536]{1,0:T(8,128)}, f32[1536,1536]{1,0:T(8,128)}, u32[]{:S(2)}, u32[]{:S(2)}) collective-permute-start(f32[1536,1536]{1,0:T(8,128)} %add.238), channel_id=1, source_target_pairs={{0,2},{1,3},{2,0},{3,1},{4,6},{5,7},{6,4},{7,5},{8,10},{9,11},{10,... | collective-permute-start | bytes 28311560 | tf_op jit(solution)/shard_map/ppermute | solution.py:130
  694.9 203.7 %copy-start.68 = (f32[1536]{0:T(1024)S(1)}, f32[1536]{0:T(1024)}, u32[]{:S(2)}) copy-start(f32[1536]{0:T(1024)} %get-tuple-element.407) | copy-start | bytes 18436
  1167.8 10.0 slice-start.16
  (83 other events, 450.3 us)
Sparse Core Ops, SparseCore 0:
  476.2 195.6 all-reduce.33
  681.8 485.9 all-reduce.31
